TPU v7x, 32 devices: a whole 2x2x4 slice. The times are simulated.
32 devices in a mesh: section: 4 (over y, x), tile: 8 (over z, core).
Axes of the slice: x: 2, y: 2, z: 4, core: 2. Of those that a mesh axis runs over, the one named last changes fastest.
Arguments:
- forcing: bfloat16 [262144, 128], P(('section', 'tile')), may hold values from -6 to 6
- w_in: bfloat16 [128, 1024], replicated, may hold values from -0.5 to 0.5
- bias_in: float32 [1024], replicated, may hold values from -3 to 3
- w_out: bfloat16 [1024, 128], replicated, may hold values from -0.1875 to 0.1875
- target_tile_index: int32 [262144, 1], P(('section', 'tile')), may hold values from 0 to 7; in each aligned block of 8192 rows (0 to 8191, 8192 to 16383, ...) at most 2048 rows name the same one
- reach_slot: int32 [262144], P(('section', 'tile')), may hold values from 0 to 63
- k_ratio: float32 [4, 512], P(None, ('section', 'tile')), may hold values from 1 to 40
- x_weight: float32 [4, 512], P(None, ('section', 'tile')), may hold values from 0.05 to 0.3
- down_link: int32 [4, 512], P(None, ('section', 'tile')), may hold values from 0 to 127
- cotangent: float32 [4, 512, 128], P(None, ('section', 'tile')), may hold values from -6 to 6
Outputs:
- discharge: float32 [4, 512, 128], P(None, ('section', 'tile'))
- grad_w_in: float32 [128, 1024], replicated
- grad_bias: float32 [1024], replicated
- grad_w_out: float32 [1024, 128], replicated
Inputs may be any that keep to these rules, and one draw needn't show every extreme that they name: `target_tile_index`: among the catchments of one device, at most 2048 name the same tile, a bound that some block reaches. `down_link`: entries of last-section reaches are not used.
All inputs are finite; a program needn't handle non-finite values.
Results may differ from a plain program's by a relative error of at most 0.0038.
Values may be sent and summed in bfloat16 or wider, within the bound.
A program may use at most 192 MiB of HBM per device.

v0:
```python
import jax
import jax.numpy as jnp
from jax import lax
from jax.sharding import PartitionSpec as P


def shifted(block, axis, distance):
    devices = range(lax.axis_size(axis))
    route = [(i - distance, i) for i in devices if i - distance in devices]
    return lax.ppermute(block, axis, route)


def coefficients(k_ratio, x_weight):
    storage = 2.0 * k_ratio * (1.0 - x_weight)
    denom = storage + 1.0
    c_now = (1.0 - 2.0 * k_ratio * x_weight) / denom
    c_prev = (1.0 + 2.0 * k_ratio * x_weight) / denom
    c_keep = (storage - 1.0) / denom
    c_side = 2.0 / denom
    return (c_now, c_prev, c_keep, c_side)


def linear_combine(first, second):
    return (first[0] * second[0], second[0] * first[1] + second[1])


def route(inflow, lateral, coefs):
    c_now, c_prev, c_keep, c_side = coefs
    before = jnp.pad(inflow[:, :, :-1], ((0, 0), (0, 0), (1, 0)))
    drive = c_now[:, :, None] * inflow + c_prev[:, :, None] * before + c_side[:, :, None] * lateral
    decay = jnp.broadcast_to(c_keep[:, :, None], drive.shape)
    _, outs = lax.associative_scan(linear_combine, (decay, drive), axis=2)
    return outs


def route_back(grad_out, coefs):
    c_now, c_prev, c_keep, c_side = coefs
    decay = jnp.broadcast_to(c_keep[:, :, None], grad_out.shape)
    _, adjoint = lax.associative_scan(linear_combine, (decay, grad_out), axis=2, reverse=True)
    after = jnp.pad(adjoint[:, :, 1:], ((0, 0), (0, 0), (0, 1)))
    grad_in = c_now[:, :, None] * adjoint + c_prev[:, :, None] * after
    grad_lat = c_side[:, :, None] * adjoint
    return (grad_in, grad_lat)


def reach_link_matrix(links, span):
    return (links[:, :, None] == jnp.arange(span, dtype=jnp.int32)[None, None, :]).astype(
        jnp.float32
    )


def pass_down(reach_outflow, links, span):
    lookup_matrix = reach_link_matrix(links, span)
    section_pieces = jnp.einsum(
        "zum,zuh->zmh", lookup_matrix, reach_outflow, precision=lax.Precision.HIGHEST
    )
    summed = lax.psum_scatter(
        section_pieces.astype(jnp.bfloat16), "tile", scatter_dimension=1, tiled=True
    ).astype(jnp.float32)
    return shifted(summed, "section", 1)


def pass_up(grad_in):
    moved = shifted(grad_in, "section", -1)
    return lax.all_gather(moved, "tile", axis=1, tiled=True)


def pick_rows(entire_network, links):
    lookup_matrix = reach_link_matrix(links, entire_network.shape[1])
    return jnp.einsum(
        "pox,pxc->poc", lookup_matrix, entire_network, precision=lax.Precision.HIGHEST
    )


def local(
    forcing,
    w_in,
    bias_in,
    w_out,
    target_tile_index,
    reach_slot,
    k_ratio,
    x_weight,
    down_link,
    cotangent,
):
    tiles = lax.axis_size("tile")
    river_sections = lax.axis_size("section")
    cells = forcing.shape[0]
    groups, reaches = k_ratio.shape
    steps_len = w_out.shape[1]
    span = tiles * reaches
    capacity = 2 * cells // tiles
    pre = jnp.dot(forcing, w_in, preferred_element_type=jnp.float32) + bias_in
    hidden = jax.nn.silu(pre).astype(jnp.bfloat16)
    runoff = (0.125 * jnp.dot(hidden, w_out, preferred_element_type=jnp.float32)).astype(
        jnp.bfloat16
    )
    target = target_tile_index[:, 0]
    onehot = (target[:, None] == jnp.arange(tiles, dtype=jnp.int32)[None, :]).astype(jnp.int32)
    rank = jnp.sum((jnp.cumsum(onehot, axis=0) - 1) * onehot, axis=1)
    position = target * capacity + rank
    send_rows = jnp.zeros((tiles * capacity, steps_len), jnp.bfloat16).at[position].set(runoff)
    send_ids = (
        jnp.full((tiles * capacity,), groups * reaches, jnp.int32).at[position].set(reach_slot)
    )
    recv_rows, recv_ids = (
        lax.all_to_all(send_rows, "tile", split_axis=0, concat_axis=0, tiled=True),
        lax.all_to_all(send_ids, "tile", split_axis=0, concat_axis=0, tiled=True),
    )
    buckets = (recv_ids[:, None] == jnp.arange(groups * reaches, dtype=jnp.int32)[None, :]).astype(
        jnp.bfloat16
    )
    lateral = lax.dot_general(
        buckets, recv_rows, (((0,), (0,)), ((), ())), preferred_element_type=jnp.float32
    )
    lateral = lateral.reshape(groups, reaches, steps_len)
    coefs = coefficients(k_ratio, x_weight)
    incoming = jnp.zeros((groups, reaches, steps_len), jnp.float32)
    for level in range(river_sections):
        discharge = route(incoming, lateral, coefs)
        if level + 1 < river_sections:
            incoming = pass_down(discharge, down_link, span)
    extra = jnp.zeros((groups, reaches, steps_len), jnp.float32)
    for level in range(river_sections):
        grad_in, grad_lateral = route_back(cotangent + extra, coefs)
        if level + 1 < river_sections:
            extra = pick_rows(pass_up(grad_in), down_link)
    flat = grad_lateral.reshape(groups * reaches, steps_len).astype(jnp.bfloat16)
    back_rows = jnp.dot(buckets, flat, preferred_element_type=jnp.float32).astype(jnp.bfloat16)
    returned = lax.all_to_all(back_rows, "tile", split_axis=0, concat_axis=0, tiled=True)
    grad_runoff = returned[position]
    grad_w_out = 0.125 * lax.dot_general(
        hidden, grad_runoff, (((0,), (0,)), ((), ())), preferred_element_type=jnp.float32
    )
    grad_hidden = 0.125 * lax.dot_general(
        grad_runoff, w_out, (((1,), (1,)), ((), ())), preferred_element_type=jnp.float32
    )
    sig = jax.nn.sigmoid(pre)
    grad_pre = grad_hidden * sig * (1.0 + pre * (1.0 - sig))
    grad_bias = jnp.sum(grad_pre, axis=0)
    grad_w_in = lax.dot_general(
        forcing,
        grad_pre.astype(jnp.bfloat16),
        (((0,), (0,)), ((), ())),
        preferred_element_type=jnp.float32,
    )
    grad_w_in, grad_bias, grad_w_out = lax.psum(
        (grad_w_in, grad_bias, grad_w_out), ("section", "tile")
    )
    return (discharge, grad_w_in, grad_bias, grad_w_out)


def solution(mesh):
    placed = (
        P(("section", "tile"), None),
        P(),
        P(),
        P(),
        P(("section", "tile"), None),
        P(("section", "tile")),
        P(None, ("section", "tile")),
        P(None, ("section", "tile")),
        P(None, ("section", "tile")),
        P(None, ("section", "tile"), None),
    )
    return jax.shard_map(
        local,
        mesh=mesh,
        in_specs=placed,
        out_specs=(P(None, ("section", "tile"), None), P(), P(), P()),
        check_vma=False,
    )
```

profile of v0, /device:TPU:0, one launch (start us, length us, event | category | flops | bytes accessed | tf_op | source)
XLA Modules:
  0.0 649.4 jit_solution(12011391910219636179)
XLA Ops:
  8.1 2.4 reduce-window.6
  13.0 31.2 %scatter_custom_fusion = s32[16384]{0:T(1024)} fusion(s32[8192]{0:T(1024)S(1)} %bitcast.132, s32[8192]{0:T(1024)} %param.15, s32[]{:T(128)} %constant.15.clone.1), kind=kCustom, calls=%fused_computation.251 | custom fusion | bytes 66048 | tf_op jit(solution)/shard_map/scatter | solution.py:105
  44.3 6.3 all-to-all-start
  58.0 19.1 %multiply_convert_fusion = (bf16[8192,1024]{1,0:T(8,128)(2,1)}, f32[8192,1024]{1,0:T(8,128)}) fusion(f32[1024]{0:T(1024)S(1)} %copy-done.7, bf16[8192,128]{1,0:T(8,128)(2,1)S(1)} %copy-done, bf16[128,1024]{1,0:T(8,128)(2,1)S(1)} %copy-done.4), kind=kOutput, calls=%fused_computation.4 | convolution fusion | flops 2197815296 | bytes 52695040 | tf_op jit(solution)/shard_map/dot_general | solution.py:94
  77.1 9.6 %fusion.2 = bf16[8192,128]{1,0:T(8,128)(2,1)} fusion(bf16[8192,1024]{1,0:T(8,128)(2,1)} %get-tuple-element.83, bf16[1024,128]{1,0:T(8,128)(2,1)S(1)} %copy-done.5), kind=kOutput, calls=%fused_computation.10 | convolution fusion | flops 2149580800 | bytes 19136512 | tf_op jit(solution)/shard_map/dot_general | solution.py:96
  86.7 24.0 %scatter_custom_fusion.1 = bf16[16384,128]{1,0:T(8,128)(2,1)} fusion(s32[8192]{0:T(1024)S(1)} %bitcast.133, bf16[8192,128]{1,0:T(8,128)(2,1)} %fusion.2, bf16[]{:T(256)} %constant.11.clone.1), kind=kCustom, calls=%fused_computation.15 | custom fusion | bytes 4194816 | tf_op jit(solution)/shard_map/scatter | solution.py:103
  110.8 5.1 all-to-all-start.1
  126.9 4.2 collective-permute-done.3
  131.1 85.7 %all_gather.9 = f32[4,128,128]{2,1,0:T(8,128)S(1)} all-gather(f32[4,16,128]{2,1,0:T(8,128)S(1)} %collective-permute-done.3), channel_id=1, replica_groups=mesh['section'=4,'tile'=8] {'tile'}, dimensions={1}, use_global_device_ids=true | all-gather | bytes 294912 | tf_op jit(solution)/shard_map/all_gather | solution.py:65
  228.3 3.1 multiply_add_fusion.13
  245.2 3.3 collective-permute-done.4
  248.6 14.4 %all_gather.10 = f32[4,128,128]{2,1,0:T(8,128)S(1)} all-gather(f32[4,16,128]{2,1,0:T(8,128)S(1)} %collective-permute-done.4), channel_id=1, replica_groups=mesh['section'=4,'tile'=8] {'tile'}, dimensions={1}, use_global_device_ids=true | all-gather | bytes 294912 | tf_op jit(solution)/shard_map/all_gather | solution.py:65
  274.2 2.8 reduce-scatter.4.cloned.1.call-done
  277.8 3.5 collective-permute-start
  281.4 1.4 collective-permute-done
  296.8 14.3 %all_gather.11 = f32[4,128,128]{2,1,0:T(8,128)S(1)} all-gather(f32[4,16,128]{2,1,0:T(8,128)S(1)} %collective-permute-done.5), channel_id=1, replica_groups=mesh['section'=4,'tile'=8] {'tile'}, dimensions={1}, use_global_device_ids=true | all-gather | bytes 294912 | tf_op jit(solution)/shard_map/all_gather | solution.py:65
  322.5 5.6 reduce-scatter.6.cloned.1.call-done
  328.9 3.6 collective-permute-start.1
  332.5 4.4 convolution_convert_fusion
  336.9 4.5 all-to-all-start.2
  354.2 33.0 %reduce-scatter.8.cloned.1.call-done = bf16[4,16,128]{2,1,0:T(8,128)(2,1)} async-done(((bf16[4,128,128]{2,1,0:T(8,128)(2,1)}), bf16[4,16,128]{2,1,0:T(8,128)(2,1)}) %reduce-scatter.8.cloned.1.call-update) | async-done | bytes 16400 | tf_op jit(solution)/shard_map/reduce_scatter | solution.py:57
  387.9 3.4 collective-permute-start.2
  391.3 1.6 collective-permute-done.2
  401.0 35.7 %all-to-all-done.2 = bf16[8,2048,128]{2,1,0:T(8,128)(2,1)} async-done(((bf16[8,2048,128]{2,1,0:T(8,128)(2,1)}), bf16[8,2048,128]{2,1,0:T(8,128)(2,1)}, u32[]{:S(2)}, u32[]{:S(2)}) %all-to-all-start.2) | async-done | bytes 4194336 | tf_op jit(solution)/shard_map/all_to_all | solution.py:131
  436.7 30.7 %gather_fusion = bf16[8192,128]{1,0:T(8,128)(2,1)} fusion(bf16[16384,128]{1,0:T(8,128)(2,1)} %bitcast.14, s32[8192]{0:T(1024)S(1)} %broadcast_clamp_fusion), kind=kCustom, calls=%fused_computation | custom fusion | bytes 4227072 | tf_op jit(solution)/shard_map/gather | solution.py:132
  467.4 11.8 %convolution_multiply_fusion.1 = f32[1024,128]{1,0:T(8,128)} fusion(bf16[8192,1024]{1,0:T(8,128)(2,1)} %get-tuple-element.83, bf16[8192,128]{1,0:T(8,128)(2,1)} %gather_fusion), kind=kOutput, calls=%fused_computation.20 | convolution fusion | flops 2147614720 | bytes 19398656 | tf_op jit(solution)/shard_map/dot_general | solution.py:133
  479.2 21.9 %fusion.84 = (f32[1024]{0:T(1024)S(1)}, bf16[8192,1024]{1,0:T(8,128)(2,1)}) fusion(f32[8192,1024]{1,0:T(8,128)} %get-tuple-element.84, f32[1024]{0:T(1024)S(1)} %copy-done.7, bf16[8192,128]{1,0:T(8,128)(2,1)S(1)} %copy-done.1, bf16[1024,128]{1,0:T(8,128)(2,1)S(1)} %copy-done.6), kind=kOutput, calls=%fused_computation.296 | convolution fusion | flops 2248145920 | bytes 52699136 | tf_op jit(solution)/shard_map/dot_general | solution.py:136
  501.1 8.9 %fusion.10 = f32[128,1024]{0,1:T(8,128)} fusion(bf16[8192,128]{1,0:T(8,128)(2,1)S(1)} %copy-done, bf16[8192,1024]{1,0:T(8,128)(2,1)} %get-tuple-element.87), kind=kOutput, calls=%fused_computation.19 | convolution fusion | flops 2147483648 | bytes 19398656 | tf_op jit(solution)/shard_map/dot_general | solution.py:142
  514.3 37.0 %psum.22 = f32[1024]{0:T(1024)} all-reduce(f32[1024]{0:T(1024)S(1)} %get-tuple-element.86), channel_id=1, replica_groups=mesh['section'=4,'tile'=8] {'section','tile'}, use_global_device_ids=true, to_apply=%region_10.11 | all-reduce | flops 1024 | bytes 8192 | tf_op jit(solution)/shard_map/psum | solution.py:148
  551.3 87.2 %all-reduce.122.cloned.1.call-done = (f32[128,1024]{0,1:T(8,128)}, f32[1024,128]{1,0:T(8,128)}) async-done(((f32[128,1024]{0,1:T(8,128)}, f32[1024,128]{1,0:T(8,128)}), (f32[128,1024]{0,1:T(8,128)}, f32[1024,128]{1,0:T(8,128)})) %all-reduce.122.cloned.1.call-update) | async-done | bytes 1048592 | tf_op jit(solution)/shard_map/psum | solution.py:148
  638.5 2.0 copy.99
  640.6 1.9 copy.104
  (540 shorter events, 109.0 us)
Async XLA Ops:
  7.2 50.8 %copy-start = (bf16[8192,128]{1,0:T(8,128)(2,1)S(1)}, bf16[8192,128]{1,0:T(8,128)(2,1)}, u32[]{:S(2)}) copy-start(bf16[8192,128]{1,0:T(8,128)(2,1)} %param.10) | copy-start | bytes 6291460
  7.2 50.8 %copy-start.4 = (bf16[128,1024]{1,0:T(8,128)(2,1)S(1)}, bf16[128,1024]{1,0:T(8,128)(2,1)}, u32[]{:S(2)}) copy-start(bf16[128,1024]{1,0:T(8,128)(2,1)} %param.11) | copy-start | bytes 786436
  7.2 50.8 %copy-start.7 = (f32[1024]{0:T(1024)S(1)}, f32[1024]{0:T(1024)}, u32[]{:S(2)}) copy-start(f32[1024]{0:T(1024)} %param.12) | copy-start | bytes 12292
  44.3 66.5 %all-to-all-start = ((s32[8,2048,1]{1,2,0:T(1,128)}), s32[8,2048,1]{1,2,0:T(1,128)S(1)}, u32[]{:S(2)}, u32[]{:S(2)}) async-start(s32[8,2048,1]{1,2,0:T(1,128)} %bitcast.5), calls=%async_computation | async-start | bytes 131072 | tf_op jit(solution)/shard_map/all_to_all | solution.py:109
  58.0 19.1 %copy-start.5 = (bf16[1024,128]{1,0:T(8,128)(2,1)S(1)}, bf16[1024,128]{1,0:T(8,128)(2,1)}, u32[]{:S(2)}) copy-start(bf16[1024,128]{1,0:T(8,128)(2,1)} %param.13) | copy-start | bytes 786436
  110.8 7.2 %copy-start.2 = (f32[4,16,128]{2,1,0:T(8,128)S(1)}, f32[4,16,128]{2,1,0:T(8,128)}, u32[]{:S(2)}) copy-start(f32[4,16,128]{2,1,0:T(8,128)} %param.19) | copy-start | bytes 98308
  110.8 117.5 %all-to-all-start.1 = ((bf16[8,2048,128]{2,1,0:T(8,128)(2,1)}), bf16[8,2048,128]{2,1,0:T(8,128)(2,1)}, u32[]{:S(2)}, u32[]{:S(2)}) async-start(bf16[8,2048,128]{2,1,0:T(8,128)(2,1)} %bitcast.89), calls=%async_computation.1 | async-start | bytes 8388608 | tf_op jit(solution)/shard_map/all_to_all | solution.py:108
  115.9 100.9 %copy-start.3 = (s32[4,16]{1,0:T(4,128)S(1)}, s32[4,16]{1,0:T(4,128)}, u32[]{:S(2)}) copy-start(s32[4,16]{1,0:T(4,128)} %param.18) | copy-start | bytes 772
  115.9 161.2 %reduce-scatter.4.cloned.1.call-start = ((), (), s32[]{:S(2)}) async-start(), calls=%async_computation.6 | async-start | bytes 147456 | tf_op jit(solution)/shard_map/reduce_scatter | solution.py:57
  125.3 5.8 collective-permute-start.3
  242.8 5.8 collective-permute-start.4
  245.2 82.9 %reduce-scatter.6.cloned.1.call-start = ((), (), s32[]{:S(2)}) async-start(), calls=%async_computation.7 | async-start | bytes 147456 | tf_op jit(solution)/shard_map/reduce_scatter | solution.py:57
  277.8 5.1 collective-permute-start
  288.0 8.8 %collective-permute-start.5 = (f32[4,16,128]{2,1,0:T(8,128)S(1)}, f32[4,16,128]{2,1,0:T(8,128)S(1)}, u32[]{:S(2)}, u32[]{:S(2)}) collective-permute-start(f32[4,16,128]{2,1,0:T(8,128)S(1)} %get-tuple-element.69), channel_id=1, source_target_pairs={{8,0},{16,8},{24,16},{9,1},{17,9},{25,17},{10,2},{18,10},{26,18},{... | collective-permute-start | bytes 98312 | tf_op jit(solution)/shard_map/ppermute | solution.py:10
  328.9 12.6 %collective-permute-start.1 = (f32[4,16,128]{2,1,0:T(8,128)S(1)}, f32[4,16,128]{2,1,0:T(8,128)S(1)}, u32[]{:S(2)}, u32[]{:S(2)}) collective-permute-start(f32[4,16,128]{2,1,0:T(8,128)S(1)} %convert_element_type.63), channel_id=1, source_target_pairs={{0,8},{8,16},{16,24},{1,9},{9,17},{17,25},{2,10},{10,18},{18,26},{... | collective-permute-start | bytes 98312 | tf_op jit(solution)/shard_map/ppermute | solution.py:10
  336.9 99.8 %all-to-all-start.2 = ((bf16[8,2048,128]{2,1,0:T(8,128)(2,1)}), bf16[8,2048,128]{2,1,0:T(8,128)(2,1)}, u32[]{:S(2)}, u32[]{:S(2)}) async-start(bf16[8,2048,128]{2,1,0:T(8,128)(2,1)} %bitcast.88), calls=%async_computation.5 | async-start | bytes 8388608 | tf_op jit(solution)/shard_map/all_to_all | solution.py:131
  341.4 45.8 %reduce-scatter.8.cloned.1.call-start = ((), (), s32[]{:S(2)}) async-start(), calls=%async_computation.8 | async-start | bytes 147456 | tf_op jit(solution)/shard_map/reduce_scatter | solution.py:57
  354.2 284.4 %all-reduce.122.cloned.1.call-start = ((), (), s32[]{:S(2)}) async-start(), calls=%async_computation.9 | async-start | bytes 2097152 | tf_op jit(solution)/shard_map/psum | solution.py:148
  387.9 4.9 collective-permute-start.2
  467.4 11.8 %copy-start.1 = (bf16[8192,128]{1,0:T(8,128)(2,1)S(1)}, bf16[8192,128]{1,0:T(8,128)(2,1)}, u32[]{:S(2)}) copy-start(bf16[8192,128]{1,0:T(8,128)(2,1)} %gather_fusion) | copy-start | bytes 6291460
  467.4 11.8 %copy-start.6 = (bf16[1024,128]{1,0:T(8,128)(2,1)S(1)}, bf16[1024,128]{1,0:T(8,128)(2,1)}, u32[]{:S(2)}) copy-start(bf16[1024,128]{1,0:T(8,128)(2,1)} %param.13) | copy-start | bytes 786436
Sparse Core Ops, SparseCore 0:
  245.3 31.6 reduce-scatter.3
  296.9 31.1 reduce-scatter.5
  354.3 32.8 reduce-scatter.7
  510.2 128.3 all-reduce.121
where the time goes:
time: 660 us; the launch traced here: 649 us
  waiting for transfers between devices  175 us (27%)
  local copies, waits for them, and re-layouts  173 us (26%)
  blocking collectives  151 us (23%)
  matrix products  82.9 us (13%)
  starting transfers between devices  30.8 us (5%)
  other arithmetic  19.5 us (3%)
  between operations  16.7 us (3%)
    all_gather x3, blocking collectives, pass_up(): return lax.all_gather(moved, 'tile', axis=1, tiled=True)  114 us
    psum x1, waiting for transfers between devices, local(): lax.psum((grad_w_in, grad_bias, grad_w_out), ('section', 'tile'))  87.2 us
    reduce_scatter x3, waiting for transfers between devices, pass_down(): lax.psum_scatter(section_pieces.astype(jnp.bfloat16), 'tile', scatter_dim...  41.4 us
    psum x1, blocking collectives, local(): lax.psum((grad_w_in, grad_bias, grad_w_out), ('section', 'tile'))  37 us
    all_to_all x1, waiting for transfers between devices, local(): lax.all_to_all(back_rows, 'tile', split_axis=0, concat_axis=0, tiled=True)  35.7 us
    scatter x1, local copies, waits for them, and re-layouts, local(): jnp.full((tiles * capacity,), groups * reaches, jnp.int32).at[position]  31.2 us
    gather x1, local copies, waits for them, and re-layouts, local(): grad_runoff = returned[position]  30.7 us
    scatter x1, local copies, waits for them, and re-layouts, local(): jnp.zeros((tiles * capacity, steps_len), jnp.bfloat16).at[position]  24 us
  transfers between devices with their start and end apart: 13, of which 9 were waited for; matrix products, arithmetic and copies ran while one was open for 22% of the time, Pallas kernels for 0%

commit v1 on v0

v1 whole, which is shorter than its diff:
```python
import functools

import jax
import jax.numpy as jnp
from jax import lax
from jax.experimental import pallas as pl
from jax.experimental.pallas import tpu as pltpu
from jax.sharding import PartitionSpec as P

F32 = jnp.float32
BF16 = jnp.bfloat16


def coefficients(k_ratio, x_weight):
    storage = 2.0 * k_ratio * (1.0 - x_weight)
    denom = storage + 1.0
    c_now = (1.0 - 2.0 * k_ratio * x_weight) / denom
    c_prev = (1.0 + 2.0 * k_ratio * x_weight) / denom
    c_keep = (storage - 1.0) / denom
    c_side = 2.0 / denom
    return (c_now, c_prev, c_keep, c_side)


def later(x, n):
    t = lax.broadcasted_iota(jnp.int32, x.shape, 0)
    return jnp.where(t >= n, pltpu.roll(x, n, 0), 0.0)


def earlier(x, n):
    t = lax.broadcasted_iota(jnp.int32, x.shape, 0)
    return jnp.where(t < x.shape[0] - n, pltpu.roll(x, x.shape[0] - n, 0), 0.0)


def scan_time(drive, decay, shift):
    n = 1
    while n < drive.shape[0]:
        drive = drive + decay * shift(drive, n)
        decay = decay * decay
        n *= 2
    return drive


def exact_dot(x, table, dims):
    total = None
    for _ in range(3):
        part = x.astype(BF16)
        x = x - part.astype(F32)
        term = lax.dot_general(part, table, (dims, ((), ())), preferred_element_type=F32)
        total = term if total is None else total + term
    return total


def section_row(params, first, groups, lanes):
    return jnp.concatenate([params[first + g : first + g + 1, lanes] for g in range(groups)], axis=1)


def section_coefs(params, groups, lanes):
    return coefficients(
        section_row(params, 0, groups, lanes), section_row(params, groups, groups, lanes)
    )


def link_table(params, g, groups, lanes, span):
    links = params[2 * groups + g : 2 * groups + g + 1, lanes]
    rows = lax.broadcasted_iota(jnp.int32, (span, span), 0).astype(F32)
    return (rows == links).astype(BF16)


def adjoint_chain(params, cot, groups, sections, span, emit):
    extra = None
    for s in reversed(range(sections)):
        lanes = slice(s * span, (s + 1) * span)
        c_now, c_prev, c_keep, c_side = section_coefs(params, groups, lanes)
        grad = jnp.concatenate([cot(g, s).T for g in range(groups)], axis=1)
        if extra is not None:
            grad = grad + extra
        adj = scan_time(grad, c_keep, earlier)
        emit(s, c_side * adj)
        if s > 0:
            grad_in = c_now * adj + c_prev * earlier(adj, 1)
            up = slice((s - 1) * span, s * span)
            extra = jnp.concatenate(
                [
                    exact_dot(
                        grad_in[:, g * span : (g + 1) * span],
                        link_table(params, g, groups, up, span),
                        ((1,), (0,)),
                    )
                    for g in range(groups)
                ],
                axis=1,
            )


def forward_chain(params, lat, groups, sections, span, emit):
    inflow = None
    for s in range(sections):
        lanes = slice(s * span, (s + 1) * span)
        c_now, c_prev, c_keep, c_side = section_coefs(params, groups, lanes)
        drive = c_side * jnp.concatenate([lat(g, s).T for g in range(groups)], axis=1)
        if inflow is not None:
            drive = drive + c_now * inflow + c_prev * later(inflow, 1)
        flow = scan_time(drive, c_keep, later)
        emit(s, flow)
        if s + 1 < sections:
            inflow = jnp.concatenate(
                [
                    exact_dot(
                        flow[:, g * span : (g + 1) * span],
                        link_table(params, g, groups, lanes, span),
                        ((1,), (1,)),
                    )
                    for g in range(groups)
                ],
                axis=1,
            )


def adjoint_kernel(groups, sections, span, params_ref, cot_ref, glat_ref):
    mine = lax.axis_index("section")

    def emit(s, glat):
        @pl.when(mine == s)
        def _():
            glat_ref[...] = 0.125 * glat.astype(BF16)

    adjoint_chain(
        params_ref[...],
        lambda g, s: cot_ref[g, s * span : (s + 1) * span, :],
        groups, sections, span, emit,
    )


def forward_kernel(groups, sections, span, params_ref, lat_ref, out_ref, flow_ref):
    mine = lax.axis_index("section")
    reaches = out_ref.shape[1]

    def emit(s, flow):
        @pl.when(mine == s)
        def _():
            for g in range(groups):
                flow_ref[g] = flow[:, g * span : (g + 1) * span].T

    forward_chain(
        params_ref[...],
        lambda g, s: lat_ref[g, s * span : (s + 1) * span, :],
        groups, sections, span, emit,
    )
    first = pl.multiple_of(lax.axis_index("tile") * reaches, 8)
    for g in range(groups):
        out_ref[g] = flow_ref[g, pl.ds(first, reaches), :]


def cells_kernel(x_ref, key_ref, w_in_ref, bias_ref, w_out_ref, glat_ref, grads_ref, lat_ref):
    feat, hid = w_in_ref.shape
    steps = w_out_ref.shape[1]
    cells = x_ref.shape[0]

    @pl.when(pl.program_id(0) == 0)
    def _():
        grads_ref[...] = jnp.zeros_like(grads_ref)
        lat_ref[...] = jnp.zeros_like(lat_ref)

    x = x_ref[...]
    pre = jnp.dot(x, w_in_ref[...], preferred_element_type=F32) + bias_ref[...]
    sig = 0.5 * jnp.tanh(0.5 * pre) + 0.5
    act = pre * sig
    slope = sig + act * (1.0 - sig)
    hidden = act.astype(BF16)
    runoff = (0.125 * jnp.dot(hidden, w_out_ref[...], preferred_element_type=F32)).astype(BF16)
    rows = lax.broadcasted_iota(jnp.int32, (lat_ref.shape[0], cells), 0)
    onehot = (rows == key_ref[...]).astype(F32).astype(BF16)
    lat_ref[...] += jnp.dot(onehot, runoff, preferred_element_type=F32)
    back = jnp.dot(glat_ref[...], onehot, preferred_element_type=F32)
    back_t = back.T.astype(BF16)
    back = back.astype(BF16)
    grads_ref[feat : feat + steps, :] += jnp.dot(back, hidden, preferred_element_type=F32)
    grad_hidden = lax.dot_general(
        back_t, w_out_ref[...], (((1,), (1,)), ((), ())), preferred_element_type=F32
    )
    grad_pre = grad_hidden * slope
    grads_ref[feat + steps : feat + steps + 1, :] += jnp.sum(grad_pre, axis=0, keepdims=True)
    grads_ref[0:feat, :] += jnp.dot(x.T, grad_pre.astype(BF16), preferred_element_type=F32)


def local(
    forcing, w_in, bias_in, w_out, target_tile_index, reach_slot,
    k_ratio, x_weight, down_link, cotangent,
):
    tiles = lax.axis_size("tile")
    sections = lax.axis_size("section")
    cells, feat = forcing.shape
    hid, steps = w_out.shape
    groups, reaches = k_ratio.shape
    span = tiles * reaches
    both = ("section", "tile")
    big = pltpu.CompilerParams(vmem_limit_bytes=56 << 20)

    own = jnp.concatenate([k_ratio, x_weight, down_link.astype(F32)], axis=0)
    params = lax.all_gather(own, both, axis=1, tiled=True)
    cot = lax.all_gather(cotangent, both, axis=1, tiled=True)
    glat = pl.pallas_call(
        functools.partial(adjoint_kernel, groups, sections, span),
        out_shape=jax.ShapeDtypeStruct((steps, groups * span), BF16),
        compiler_params=big,
    )(params, cot)

    key = (reach_slot // reaches) * span + target_tile_index[:, 0] * reaches + reach_slot % reaches
    block = min(cells, 1024)
    whole = lambda shape: pl.BlockSpec(shape, lambda i: (0, 0))
    grads, lateral = pl.pallas_call(
        cells_kernel,
        grid=(cells // block,),
        in_specs=[
            pl.BlockSpec((block, feat), lambda i: (i, 0)),
            pl.BlockSpec((1, block), lambda i: (0, i)),
            whole((feat, hid)), whole((1, hid)), whole((hid, steps)), whole((steps, groups * span)),
        ],
        out_specs=[whole((feat + steps + 8, hid)), whole((groups * span, steps))],
        out_shape=[
            jax.ShapeDtypeStruct((feat + steps + 8, hid), F32),
            jax.ShapeDtypeStruct((groups * span, steps), F32),
        ],
        compiler_params=big,
    )(forcing, key[None, :], w_in, bias_in[None, :], w_out, glat)

    lateral = lax.psum(lateral, "tile").reshape(groups, span, steps)
    lateral = lax.all_gather(lateral, "section", axis=1, tiled=True)
    discharge = pl.pallas_call(
        functools.partial(forward_kernel, groups, sections, span),
        out_shape=jax.ShapeDtypeStruct((groups, reaches, steps), F32),
        scratch_shapes=[pltpu.VMEM((groups, span, steps), F32)],
        compiler_params=big,
    )(params, lateral)
    grads = lax.psum(grads, both)
    return (discharge, grads[:feat], grads[feat + steps], grads[feat : feat + steps].T)


def solution(mesh):
    placed = (
        P(("section", "tile"), None),
        P(),
        P(),
        P(),
        P(("section", "tile"), None),
        P(("section", "tile")),
        P(None, ("section", "tile")),
        P(None, ("section", "tile")),
        P(None, ("section", "tile")),
        P(None, ("section", "tile"), None),
    )
    return jax.shard_map(
        local,
        mesh=mesh,
        in_specs=placed,
        out_specs=(P(None, ("section", "tile"), None), P(), P(), P()),
        check_vma=False,
    )
```

time: 660 us -> 331 us (0.50); the launches traced: 649 us -> 331 us
  local copies, waits for them, and re-layouts: 173 us -> 5.23 us
  blocking collectives: 151 us -> 44.3 us
  matrix products: 82.9 us -> 0 us
  waiting for transfers between devices: 175 us -> 223 us
  Pallas kernels: 0 us -> 40.5 us
  starting transfers between devices: 30.8 us -> 0.16 us
  other arithmetic: 19.5 us -> 3.59 us
    psum x1 -> x2, waiting for transfers between devices: 87.2 us -> 189 us  [the longest x1 135 us: local(): grads = lax.psum(grads, both)]
    dot_general x13 -> x0, matrix products: 82.9 us -> none  [the longest x1 21.9 us: local(): lax.dot_general(grad_runoff, w_out, (((1,), (1,)), ((), ())), preferred_e...]
    all_gather x3 -> x1, blocking collectives: 114 us -> 44.3 us  [local(): params = lax.all_gather(own, both, axis=1, tiled=True)]
    scatter x2 -> x0, local copies, waits for them, and re-layouts: 55.3 us -> none  [the longest x1 31.2 us: local(): jnp.full((tiles * capacity,), groups * reaches, jnp.int32).at[position]]
    pad x97 -> x0, local copies, waits for them, and re-layouts: 42.7 us -> none  [the longest x48 21.5 us: route(): _, outs = lax.associative_scan(linear_combine, (decay, drive), axis=2)]
    reduce_scatter x3 -> x0, waiting for transfers between devices: 41.4 us -> none  [pass_down(): lax.psum_scatter(section_pieces.astype(jnp.bfloat16), 'tile', scatter_dim...]
    pallas_call x0 -> x3, Pallas kernels: none -> 40.5 us  [the longest x1 33.2 us: local(): pl.pallas_call(cells_kernel, grid=(cells // block,), in_specs=[pl.BlockSp...]
    slice x175 -> x1, local copies, waits for them, and re-layouts: 40 us -> 1.35 us  [local(): grads[feat + steps]]
  transfers between devices with their start and end apart: 13 -> 4, of which waited for: 9 -> 4; matrix products, arithmetic and copies ran while one was open for 22% -> 3% of each run, Pallas kernels for 0% -> 0%
where the time goes in v1:
time: 331 us
  waiting for transfers between devices  223 us (67%)
  blocking collectives  44.3 us (13%)
  Pallas kernels  40.5 us (12%)
  between operations  13.8 us (4%)
  local copies, waits for them, and re-layouts  5.23 us (2%)
  other arithmetic  3.59 us (1%)
    psum x1, waiting for transfers between devices, local(): grads = lax.psum(grads, both)  135 us
    psum x1, waiting for transfers between devices, local(): lateral = lax.psum(lateral, 'tile').reshape(groups, span, steps)  54 us
    all_gather x1, blocking collectives, local(): params = lax.all_gather(own, both, axis=1, tiled=True)  44.3 us
    pallas_call x1, Pallas kernels, local(): pl.pallas_call(cells_kernel, grid=(cells // block,), in_specs=[pl.BlockSp...  33.2 us
    all_gather x1, waiting for transfers between devices, local(): lateral = lax.all_gather(lateral, 'section', axis=1, tiled=True)  24.1 us
    all_gather x1, waiting for transfers between devices, local(): cot = lax.all_gather(cotangent, both, axis=1, tiled=True)  8.71 us
  transfers between devices with their start and end apart: 4, of which 4 were waited for; matrix products, arithmetic and copies ran while one was open for 3% of the time, Pallas kernels for 0%

profile of v1, /device:TPU:0, one launch (start us, length us, event | category | flops | bytes accessed | tf_op | source)
XLA Modules:
  0.0 331.0 jit_solution(3964212174281492946)
XLA Ops:
  7.2 0.0 all-gather.3.cloned.1.call-start
  7.2 0.7 all-gather.3.cloned.1.call-update
  7.9 0.0 all-reduce.3.cloned.1.call-start
  7.9 0.7 convert_element_type.3
  8.6 0.7 pad_maximum_fusion
  9.3 0.1 copy.21
  9.4 44.3 %all_gather.9 = f32[12,512]{0,1:T(8,128)S(1)} all-gather(f32[12,16]{0,1:T(8,128)S(1)} %copy.21), channel_id=1, replica_groups=mesh['section'=4,'tile'=8] {'section','tile'}, dimensions={1}, use_global_device_ids=true | all-gather | bytes 25344 | tf_op jit(solution)/shard_map/all_gather | solution.py:200
  53.7 0.7 copy.23.params_ref
  54.5 0.8 broadcast_multiply_fusion
  55.2 1.4 fusion.2
  56.7 8.7 %all-gather.3.cloned.1.call-done.cot_ref = f32[4,512,128]{2,1,0:T(8,128)} async-done(((f32[4,16,128]{2,1,0:T(8,128)}), f32[4,512,128]{2,1,0:T(8,128)}) %all-gather.3.cloned.1.call-update) | async-done | bytes 1048592 | tf_op jit(solution)/shard_map/all_gather | solution.py:201
  65.4 3.4 %shard_map.129.glat_ref = bf16[128,512]{1,0:T(8,128)(2,1)} custom-call(f32[12,512]{1,0:T(8,128)} %copy.23.params_ref, f32[4,512,128]{2,1,0:T(8,128)} %all-gather.3.cloned.1.call-done.cot_ref), custom_call_target="tpu_custom_call" | custom-call | tf_op jit(solution)/shard_map/pallas_call | solution.py:202
  68.8 33.2 %shard_map.130 = (f32[264,1024]{1,0:T(8,128)}, f32[512,128]{1,0:T(8,128)}) custom-call(bf16[8192,128]{1,0:T(8,128)(2,1)} %x_ref.1, s32[1,8192]{1,0:T(1,128)} %bitcast.8, bf16[128,1024]{1,0:T(8,128)(2,1)} %w_in_ref.1, f32[1,1024]{1,0:T(1,128)} %bitcast.10, bf16[1024,128]{1,0:T(8,128)(2,1)} %w_out_ref.1, bf16[128,512]{1,0:T(8,128)(2,1)} %shard_map.129.glat_ref), custom_call_target="tpu_custom_call" | custom-call | tf_op jit(solution)/shard_map/pallas_call | solution.py:211
  102.0 0.0 all-reduce.3.cloned.1.call-update
  102.0 0.0 all-reduce.5.cloned.1.call-start
  102.1 0.7 all-reduce.5.cloned.1.call-update
  102.8 0.0 all-gather.5.cloned.1.call-start
  102.8 54.0 %all-reduce.3.cloned.1.call-done = f32[4,128,128]{2,1,0:T(8,128)} async-done(((f32[4,128,128]{2,1,0:T(8,128)}), f32[4,128,128]{2,1,0:T(8,128)}) %all-reduce.3.cloned.1.call-update) | async-done | bytes 262160 | tf_op jit(solution)/shard_map/psum | solution.py:227
  156.8 0.0 all-gather.5.cloned.1.call-update
  156.8 135.2 %all-reduce.5.cloned.1.call-done = f32[264,1024]{1,0:T(8,128)} async-done(((f32[264,1024]{1,0:T(8,128)}), f32[264,1024]{1,0:T(8,128)}) %all-reduce.5.cloned.1.call-update) | async-done | bytes 1081360 | tf_op jit(solution)/shard_map/psum | solution.py:235
  292.0 2.1 slice_bitcast_fusion
  294.1 1.0 copy.24
  295.1 1.4 slice.13
  296.4 24.1 %all-gather.5.cloned.1.call-done.lat_ref = f32[4,512,128]{2,1,0:T(8,128)} async-done(((f32[4,128,128]{2,1,0:T(8,128)}), f32[4,512,128]{2,1,0:T(8,128)}) %all-gather.5.cloned.1.call-update) | async-done | bytes 1048592 | tf_op jit(solution)/shard_map/all_gather | solution.py:228
  320.6 3.9 %shard_map.131 = f32[4,16,128]{2,1,0:T(8,128)} custom-call(f32[12,512]{1,0:T(8,128)} %copy.23.params_ref, f32[4,512,128]{2,1,0:T(8,128)} %all-gather.5.cloned.1.call-done.lat_ref), custom_call_target="tpu_custom_call" | custom-call | tf_op jit(solution)/shard_map/pallas_call | solution.py:229
Async XLA Ops:
  7.2 58.2 %all-gather.3.cloned.1.call-start = ((), (), s32[]{:S(2)}) async-start(), calls=%async_computation | async-start | bytes 1081344 | tf_op jit(solution)/shard_map/all_gather | solution.py:201
  7.9 148.9 %all-reduce.3.cloned.1.call-start = ((), (), s32[]{:S(2)}) async-start(), calls=%async_computation.1 | async-start | bytes 524288 | tf_op jit(solution)/shard_map/psum | solution.py:227
  102.0 190.0 %all-reduce.5.cloned.1.call-start = ((), (), s32[]{:S(2)}) async-start(), calls=%async_computation.3 | async-start | bytes 2162688 | tf_op jit(solution)/shard_map/psum | solution.py:235
  102.8 217.8 %all-gather.5.cloned.1.call-start = ((), (), s32[]{:S(2)}) async-start(), calls=%async_computation.2 | async-start | bytes 1310720 | tf_op jit(solution)/shard_map/all_gather | solution.py:228
Sparse Core Ops, SparseCore 0:
  10.9 54.4 all-gather.2
  102.1 54.5 all-reduce.2
  163.1 128.8 all-reduce.4
  293.7 26.8 all-gather.4

commit v2 on v1

v2 whole, which is shorter than its diff:
```python
import functools

import jax
import jax.numpy as jnp
from jax import lax
from jax.experimental import pallas as pl
from jax.experimental.pallas import tpu as pltpu
from jax.sharding import PartitionSpec as P

F32 = jnp.float32
BF16 = jnp.bfloat16


def coefficients(k_ratio, x_weight):
    storage = 2.0 * k_ratio * (1.0 - x_weight)
    denom = storage + 1.0
    c_now = (1.0 - 2.0 * k_ratio * x_weight) / denom
    c_prev = (1.0 + 2.0 * k_ratio * x_weight) / denom
    c_keep = (storage - 1.0) / denom
    c_side = 2.0 / denom
    return (c_now, c_prev, c_keep, c_side)


def later(x, n):
    t = lax.broadcasted_iota(jnp.int32, x.shape, 0)
    return jnp.where(t >= n, pltpu.roll(x, n, 0), 0.0)


def earlier(x, n):
    t = lax.broadcasted_iota(jnp.int32, x.shape, 0)
    return jnp.where(t < x.shape[0] - n, pltpu.roll(x, x.shape[0] - n, 0), 0.0)


def scan_time(drive, decay, shift):
    n = 1
    while n < drive.shape[0]:
        drive = drive + decay * shift(drive, n)
        decay = decay * decay
        n *= 2
    return drive


def exact_dot(x, table, dims):
    total = None
    for _ in range(3):
        part = x.astype(BF16)
        x = x - part.astype(F32)
        term = lax.dot_general(part, table, (dims, ((), ())), preferred_element_type=F32)
        total = term if total is None else total + term
    return total


def joined(parts):
    return jnp.concatenate(parts, axis=1)


def section_coefs(rows, groups):
    k_ratio = joined([rows[g : g + 1] for g in range(groups)])
    x_weight = joined([rows[groups + g : groups + g + 1] for g in range(groups)])
    return coefficients(k_ratio, x_weight)


def by_link(x, rows, groups, span, dims):
    spots = lax.broadcasted_iota(jnp.int32, (span, span), 0).astype(F32)
    out = []
    for g in range(groups):
        table = (spots == rows[2 * groups + g : 2 * groups + g + 1]).astype(F32).astype(BF16)
        out.append(exact_dot(x[:, g * span : (g + 1) * span], table, dims))
    return joined(out)


def adjoint_chain(rows, cot, groups, sections, span, emit):
    extra = None
    for s in reversed(range(sections)):
        c_now, c_prev, c_keep, c_side = section_coefs(rows(s), groups)
        grad = joined([cot(g, s).T for g in range(groups)])
        if extra is not None:
            grad = grad + extra
        adj = scan_time(grad, c_keep, earlier)
        emit(s, c_side * adj)
        if s > 0:
            grad_in = c_now * adj + c_prev * earlier(adj, 1)
            extra = by_link(grad_in, rows(s - 1), groups, span, ((1,), (0,)))


def forward_chain(rows, lat, groups, sections, span, emit):
    inflow = None
    for s in range(sections):
        own = rows(s)
        c_now, c_prev, c_keep, c_side = section_coefs(own, groups)
        drive = c_side * joined([lat(g, s).T for g in range(groups)])
        if inflow is not None:
            drive = drive + c_now * inflow + c_prev * later(inflow, 1)
        flow = scan_time(drive, c_keep, later)
        emit(s, flow)
        if s + 1 < sections:
            inflow = by_link(flow, own, groups, span, ((1,), (1,)))


def step_kernel(
    groups, sections, tiles, reaches, block,
    x_ref, key_ref, w_in_ref, bias_ref, w_out_ref, own_ref,
    flow_out, w_in_out, bias_out, w_out_out,
    hidden_ref, slope_ref, cot_ref, lat_ref, lat_part, lat_all, glat_ref, grads_ref, bias_acc,
    flow_ref, ws_ref, wr1, wsum, ws2, wr2, wg, br1, br2, bias_sum,
    sec_send, sec_recv, tile_send, tile_recv,
):
    span = tiles * reaches
    slots = groups * reaches
    n_blocks = x_ref.shape[0] // block
    feat, hid = w_in_ref.shape
    steps = w_out_ref.shape[1]
    chunk_rows, chunk_cols = wg.shape[2:]
    col_split = hid // chunk_cols
    sec, tile = lax.axis_index("section"), lax.axis_index("tile")

    barrier = pltpu.get_barrier_semaphore()
    for axis, me, n in (("section", sec, sections), ("tile", tile, tiles)):
        for d in range(1, n):
            pl.semaphore_signal(
                barrier, inc=1, device_id={axis: lax.rem(me + d, n)},
                device_id_type=pl.DeviceIdType.MESH,
            )
    pl.semaphore_wait(barrier, sections + tiles - 2)

    def push(axis, phase, src, dst):
        me, n, send, recv = (
            (sec, sections, sec_send, sec_recv)
            if axis == "section"
            else (tile, tiles, tile_send, tile_recv)
        )
        copies = []
        for d in range(1, n):
            peer = lax.rem(me + d, n)
            copy = pltpu.make_async_remote_copy(
                src_ref=src(peer), dst_ref=dst(d), send_sem=send.at[phase, d],
                recv_sem=recv.at[phase, d], device_id={axis: peer},
                device_id_type=pl.DeviceIdType.MESH,
            )
            copy.start()
            copies.append(copy)
        return copies

    def finish(copies):
        for copy in copies:
            copy.wait()

    cot_ref[sec, tile] = own_ref[...]
    mine = lambda _: cot_ref.at[sec, tile]
    moving = push("tile", 0, mine, mine)

    lat_part[...] = jnp.zeros_like(lat_part)
    grads_ref[...] = jnp.zeros_like(grads_ref)
    bias_acc[...] = jnp.zeros_like(bias_acc)

    def onehot(i):
        rows = lax.broadcasted_iota(jnp.int32, (groups * span, block), 0)
        return (rows == key_ref[i]).astype(F32).astype(BF16)

    def ahead(i, _):
        at = pl.ds(pl.multiple_of(i * block, block), block)
        pre = jnp.dot(x_ref[at, :], w_in_ref[...], preferred_element_type=F32) + bias_ref[...]
        sig = 0.5 * jnp.tanh(0.5 * pre) + 0.5
        act = pre * sig
        slope_ref[at, :] = (sig + act * (1.0 - sig)).astype(BF16)
        hidden = act.astype(BF16)
        hidden_ref[at, :] = hidden
        runoff = (0.125 * jnp.dot(hidden, w_out_ref[...], preferred_element_type=F32)).astype(BF16)
        part = jnp.dot(onehot(i), runoff, preferred_element_type=F32)
        lat_part[...] += part.reshape(lat_part.shape)
        return 0

    def behind(i, _):
        at = pl.ds(pl.multiple_of(i * block, block), block)
        back = jnp.dot(glat_ref[...], onehot(i), preferred_element_type=F32)
        back_t = back.T.astype(BF16)
        grads_ref[feat : feat + steps, :] += jnp.dot(
            back.astype(BF16), hidden_ref[at, :], preferred_element_type=F32
        )
        grad_hidden = lax.dot_general(
            back_t, w_out_ref[...], (((1,), (1,)), ((), ())), preferred_element_type=F32
        )
        grad_pre = grad_hidden * slope_ref[at, :].astype(F32)
        bias_acc[...] += jnp.sum(grad_pre, axis=0, keepdims=True)
        grads_ref[0:feat, :] += jnp.dot(
            x_ref[at, :].T, grad_pre.astype(BF16), preferred_element_type=F32
        )
        return 0

    half = n_blocks // 2
    lax.fori_loop(0, half, ahead, 0)
    finish(moving)
    mine = lambda _: cot_ref.at[sec]
    moving = push("section", 0, mine, mine)
    lax.fori_loop(half, n_blocks, ahead, 0)
    finish(moving)
    moving = push("tile", 1, lambda peer: lat_part.at[:, peer], lambda d: lat_ref.at[d])

    rows = lambda s: cot_ref[s, :, slots:, :].reshape(span, steps).T

    def emit_glat(s, glat):
        @pl.when(sec == s)
        def _():
            glat_ref[...] = (0.125 * glat.astype(BF16).astype(F32)).astype(BF16)

    adjoint_chain(
        rows,
        lambda g, s: cot_ref[s, :, g * reaches : (g + 1) * reaches, :].reshape(span, steps),
        groups, sections, span, emit_glat,
    )

    finish(moving)
    total = lat_part[:, tile]
    for d in range(1, tiles):
        total = total + lat_ref[d]
    lat_all[sec, tile] = total
    mine = lambda _: lat_all.at[sec, tile]
    moving = push("tile", 2, mine, mine)
    lax.fori_loop(0, half, behind, 0)
    finish(moving)
    mine = lambda _: lat_all.at[sec]
    moving = push("section", 1, mine, mine)
    lax.fori_loop(half, n_blocks, behind, 0)
    finish(moving)

    def spot(c):
        r, w = c // col_split * chunk_rows, c % col_split * chunk_cols
        return slice(r, r + chunk_rows), slice(w, w + chunk_cols)

    for s in range(sections):
        for t in range(tiles):
            ws_ref[s, t] = grads_ref[spot(s * tiles + t)].astype(BF16)
    moving = push("section", 2, lambda peer: ws_ref.at[peer], lambda d: wr1.at[d])
    moving += push("section", 3, lambda _: bias_acc, lambda d: br1.at[d])

    def emit_flow(s, flow):
        @pl.when(sec == s)
        def _():
            for g in range(groups):
                flow_ref[g] = flow[:, g * span : (g + 1) * span].T.reshape(tiles, reaches, steps)

    forward_chain(
        rows,
        lambda g, s: lat_all[s, :, g].reshape(span, steps),
        groups, sections, span, emit_flow,
    )
    flow_out[...] = flow_ref[:, tile]

    finish(moving)
    total = ws_ref[sec].astype(F32)
    bias = bias_acc[...]
    for d in range(1, sections):
        total = total + wr1[d].astype(F32)
        bias = bias + br1[d]
    wsum[...] = total
    ws2[...] = total.astype(BF16)
    bias_sum[...] = bias
    moving = push("tile", 3, lambda peer: ws2.at[peer], lambda d: wr2.at[d])
    moving += push("tile", 4, lambda _: bias_sum, lambda d: br2.at[d])
    finish(moving)
    total = wsum[tile]
    for d in range(1, tiles):
        total = total + wr2[d].astype(F32)
        bias = bias + br2[d]
    wg[sec, tile] = total.astype(BF16)
    mine = lambda _: wg.at[sec, tile]
    moving = push("tile", 5, mine, mine)
    bias_out[...] = bias
    finish(moving)
    mine = lambda _: wg.at[sec]
    moving = push("section", 4, mine, mine)
    finish(moving)
    for s in range(sections):
        for t in range(tiles):
            grads_ref[spot(s * tiles + t)] = wg[s, t].astype(F32)
    w_in_out[...] = grads_ref[0:feat, :]
    w_out_out[...] = grads_ref[feat : feat + steps, :].T


def local(
    forcing, w_in, bias_in, w_out, target_tile_index, reach_slot,
    k_ratio, x_weight, down_link, cotangent,
):
    tiles = lax.axis_size("tile")
    sections = lax.axis_size("section")
    cells, feat = forcing.shape
    hid, steps = w_out.shape
    groups, reaches = k_ratio.shape
    span = tiles * reaches
    slots = groups * reaches
    block = min(cells // 2, 512)
    chunks = sections * tiles
    chunk_rows = 8
    chunk_cols = (feat + steps) * hid // (chunks * chunk_rows)

    own = jnp.concatenate([k_ratio, x_weight, down_link.astype(F32)], axis=0).T
    own = jnp.pad(own, ((0, 0), (0, steps - own.shape[1])))
    own = jnp.concatenate([cotangent.reshape(slots, steps), own], axis=0)
    key = (reach_slot // reaches) * span + target_tile_index[:, 0] * reaches + reach_slot % reaches

    vmem = pl.BlockSpec(memory_space=pltpu.VMEM)
    part = (chunk_rows, chunk_cols)
    flow, g_in, g_bias, g_out = pl.pallas_call(
        functools.partial(step_kernel, groups, sections, tiles, reaches, block),
        in_specs=[vmem] * 6,
        out_specs=[vmem] * 4,
        out_shape=[
            jax.ShapeDtypeStruct((groups, reaches, steps), F32),
            jax.ShapeDtypeStruct((feat, hid), F32),
            jax.ShapeDtypeStruct((1, hid), F32),
            jax.ShapeDtypeStruct((hid, steps), F32),
        ],
        scratch_shapes=[
            pltpu.VMEM((cells, hid), BF16),
            pltpu.VMEM((cells, hid), BF16),
            pltpu.VMEM((sections, tiles, slots + reaches, steps), F32),
            pltpu.VMEM((tiles, groups, reaches, steps), F32),
            pltpu.VMEM((groups, tiles, reaches, steps), F32),
            pltpu.VMEM((sections, tiles, groups, reaches, steps), F32),
            pltpu.VMEM((steps, groups * span), BF16),
            pltpu.VMEM((feat + steps, hid), F32),
            pltpu.VMEM((1, hid), F32),
            pltpu.VMEM((groups, tiles, reaches, steps), F32),
            pltpu.VMEM((sections, tiles) + part, BF16),
            pltpu.VMEM((sections, tiles) + part, BF16),
            pltpu.VMEM((tiles,) + part, F32),
            pltpu.VMEM((tiles,) + part, BF16),
            pltpu.VMEM((tiles,) + part, BF16),
            pltpu.VMEM((sections, tiles) + part, BF16),
            pltpu.VMEM((sections, 1, hid), F32),
            pltpu.VMEM((tiles, 1, hid), F32),
            pltpu.VMEM((1, hid), F32),
            pltpu.SemaphoreType.DMA((5, sections)),
            pltpu.SemaphoreType.DMA((5, sections)),
            pltpu.SemaphoreType.DMA((6, tiles)),
            pltpu.SemaphoreType.DMA((6, tiles)),
        ],
        compiler_params=pltpu.CompilerParams(
            vmem_limit_bytes=60 << 20, collective_id=0, has_side_effects=True
        ),
    )(forcing, key.reshape(cells // block, 1, block), w_in, bias_in[None, :], w_out, own)
    return (flow, g_in, g_bias[0], g_out)


def solution(mesh):
    placed = (
        P(("section", "tile"), None),
        P(),
        P(),
        P(),
        P(("section", "tile"), None),
        P(("section", "tile")),
        P(None, ("section", "tile")),
        P(None, ("section", "tile")),
        P(None, ("section", "tile")),
        P(None, ("section", "tile"), None),
    )
    return jax.shard_map(
        local,
        mesh=mesh,
        in_specs=placed,
        out_specs=(P(None, ("section", "tile"), None), P(), P(), P()),
        check_vma=False,
    )
```

time: 331 us -> 103 us (0.31)
  waiting for transfers between devices: 223 us -> 0 us
  Pallas kernels: 40.5 us -> 89.8 us
  blocking collectives: 44.3 us -> 0 us
  between operations: 13.8 us -> 0.65 us
    psum x2 -> x0, waiting for transfers between devices: 189 us -> none  [the longest x1 135 us: local(): grads = lax.psum(grads, both)]
    pallas_call x3 -> x1, Pallas kernels: 40.5 us -> 89.8 us  [local(): pl.pallas_call(functools.partial(step_kernel, groups, sections, tiles, re...]
    all_gather x1 -> x0, blocking collectives: 44.3 us -> none  [local(): params = lax.all_gather(own, both, axis=1, tiled=True)]
    all_gather x2 -> x0, waiting for transfers between devices: 32.8 us -> none  [the longest x1 24.1 us: local(): lateral = lax.all_gather(lateral, 'section', axis=1, tiled=True)]
    unnamed x1 -> x6, local copies, waits for them, and re-layouts: 0.99 us -> 7.91 us
  transfers between devices with their start and end apart: 4 -> 0, of which waited for: 4 -> 0; matrix products, arithmetic and copies ran while one was open for 3% -> 0% of each run, Pallas kernels for 0% -> 0%
where the time goes in v2:
time: 103 us
  Pallas kernels  89.8 us (87%)
  local copies, waits for them, and re-layouts  8 us (8%)
  other arithmetic  4.34 us (4%)
    pallas_call x1, Pallas kernels, local(): pl.pallas_call(functools.partial(step_kernel, groups, sections, tiles, re...  89.8 us
    unnamed x6, local copies, waits for them, and re-layouts  7.91 us

profile of v2, /device:TPU:0, one launch (start us, length us, event | category | flops | bytes accessed | tf_op | source)
XLA Modules:
  0.0 102.8 jit_solution(2544289638369809199)
XLA Ops:
  0.6 0.7 convert_element_type.5
  1.3 0.1 copy.19
  1.4 0.8 copy.17
  2.2 0.8 copy.18
  2.9 0.1 maximum_bitcast_fusion
  3.0 1.4 %select_maximum_fusion.own_ref = f32[80,128]{1,0:T(8,128)} fusion(f32[16,12]{1,0:T(8,128)S(1)} %maximum_bitcast_fusion, f32[64,128]{1,0:T(8,128)} %bitcast.9), kind=kLoop, calls=%fused_computation.5 | loop fusion | flops 30720 | bytes 74496 | tf_op jit(solution)/shard_map/concatenate | solution.py:298
  4.4 0.8 broadcast_multiply_fusion
  5.2 1.4 %fusion.2 = s32[8192]{0:T(1024)} fusion(s32[8192]{0:T(1024)S(1)} %bitcast.8, s32[8192]{0:T(1024)} %param.15), kind=kLoop, calls=%fused_computation.9 | loop fusion | flops 180224 | bytes 98304 | tf_op jit(solution)/shard_map/add | solution.py:299
  6.6 89.8 %shard_map.129 = (f32[4,16,128]{2,1,0:T(8,128)}, f32[128,1024]{1,0:T(8,128)}, f32[1,1024]{1,0:T(1,128)}, f32[1024,128]{1,0:T(8,128)}) custom-call(bf16[8192,128]{1,0:T(8,128)(2,1)} %x_ref.1, s32[16,1,512]{2,1,0:T(1,128)} %bitcast.7, bf16[128,1024]{1,0:T(8,128)(2,1)} %w_in_ref.1, f32[1,1024]{1,0:T(1,128)} %bitcast.10, bf16[1024,128]{1,0:T(8,128)(2,1)} %w_out_ref.1, ...), custom_call_target="tpu_custom_call" | custom-call | tf_op jit(solution)/shard_map/pallas_call | solution.py:303
  96.4 1.4 %copy.24 = f32[4,16,128]{2,1,0:T(8,128)} copy(f32[4,16,128]{2,1,0:T(8,128)} %get-tuple-element.16) | data formatting | bytes 65536
  97.8 1.9 %copy.25 = f32[128,1024]{1,0:T(8,128)} copy(f32[128,1024]{1,0:T(8,128)} %get-tuple-element.17) | data formatting | bytes 1048576
  99.7 1.3 %copy.26 = f32[1024]{0:T(1024)} copy(f32[1024]{0:T(1024)} %bitcast.11) | data formatting | bytes 8192
  101.0 1.9 %copy.27 = f32[1024,128]{1,0:T(8,128)} copy(f32[1024,128]{1,0:T(8,128)} %get-tuple-element.19) | data formatting | bytes 1048576

commit v3 on v2

v3 whole, which is shorter than its diff:
```python
import functools

import jax
import jax.numpy as jnp
from jax import lax
from jax.experimental import pallas as pl
from jax.experimental.pallas import tpu as pltpu
from jax.sharding import PartitionSpec as P

F32 = jnp.float32
BF16 = jnp.bfloat16


def coefficients(k_ratio, x_weight):
    storage = 2.0 * k_ratio * (1.0 - x_weight)
    denom = storage + 1.0
    c_now = (1.0 - 2.0 * k_ratio * x_weight) / denom
    c_prev = (1.0 + 2.0 * k_ratio * x_weight) / denom
    c_keep = (storage - 1.0) / denom
    c_side = 2.0 / denom
    return (c_now, c_prev, c_keep, c_side)


def later(x, n):
    t = lax.broadcasted_iota(jnp.int32, x.shape, 0)
    return jnp.where(t >= n, pltpu.roll(x, n, 0), 0.0)


def earlier(x, n):
    t = lax.broadcasted_iota(jnp.int32, x.shape, 0)
    return jnp.where(t < x.shape[0] - n, pltpu.roll(x, x.shape[0] - n, 0), 0.0)


def scan_time(drive, decay, shift):
    n = 1
    while n < drive.shape[0]:
        drive = drive + decay * shift(drive, n)
        decay = decay * decay
        n *= 2
    return drive


def exact_dot(x, table, dims):
    total = None
    for _ in range(3):
        part = x.astype(BF16)
        x = x - part.astype(F32)
        term = lax.dot_general(part, table, (dims, ((), ())), preferred_element_type=F32)
        total = term if total is None else total + term
    return total


def joined(parts):
    return jnp.concatenate(parts, axis=1)


def section_coefs(rows, groups):
    k_ratio = joined([rows[g : g + 1] for g in range(groups)])
    x_weight = joined([rows[groups + g : groups + g + 1] for g in range(groups)])
    return coefficients(k_ratio, x_weight)


def by_link(x, rows, groups, span, dims):
    spots = lax.broadcasted_iota(jnp.int32, (span, span), 0).astype(F32)
    out = []
    for g in range(groups):
        table = (spots == rows[2 * groups + g : 2 * groups + g + 1]).astype(F32).astype(BF16)
        out.append(exact_dot(x[:, g * span : (g + 1) * span], table, dims))
    return joined(out)


def adjoint_chain(rows, cot, groups, sections, span, emit):
    extra = None
    for s in reversed(range(sections)):
        c_now, c_prev, c_keep, c_side = section_coefs(rows(s), groups)
        grad = joined([cot(g, s).T for g in range(groups)])
        if extra is not None:
            grad = grad + extra
        adj = scan_time(grad, c_keep, earlier)
        emit(s, c_side * adj)
        if s > 0:
            grad_in = c_now * adj + c_prev * earlier(adj, 1)
            extra = by_link(grad_in, rows(s - 1), groups, span, ((1,), (0,)))


def forward_chain(rows, lat, groups, sections, span, emit):
    inflow = None
    for s in range(sections):
        own = rows(s)
        c_now, c_prev, c_keep, c_side = section_coefs(own, groups)
        drive = c_side * joined([lat(g, s).T for g in range(groups)])
        if inflow is not None:
            drive = drive + c_now * inflow + c_prev * later(inflow, 1)
        flow = scan_time(drive, c_keep, later)
        emit(s, flow)
        if s + 1 < sections:
            inflow = by_link(flow, own, groups, span, ((1,), (1,)))


def step_kernel(
    groups, sections, tiles, reaches, block,
    x_ref, target_ref, slot_ref, w_in_ref, bias_ref, w_out_ref, k_ref, weight_ref, link_ref, own_ref,
    flow_out, bias_out, wg_out, side_ref,
    hidden_ref, slope_ref, back_ref, cot_ref, lat_ref, lat_part, lat_all, glat_ref, grads_ref,
    bias_acc, flow_ref, ws_ref, wr1, ws2, wr2, wg, br1, br2, bias_sum,
    sec_send, sec_recv, tile_send, tile_recv,
):
    span = tiles * reaches
    slots = groups * reaches
    n_blocks = x_ref.shape[0] // block
    feat, hid = w_in_ref.shape
    steps = w_out_ref.shape[1]
    sec, tile = lax.axis_index("section"), lax.axis_index("tile")
    chips = tiles // 2
    chip, core = tile // 2, lax.rem(tile, 2)

    barrier = pltpu.get_barrier_semaphore()
    for axis, me, n in (("section", sec, sections), ("tile", tile, tiles)):
        for d in range(1, n):
            pl.semaphore_signal(
                barrier, inc=1, device_id={axis: lax.rem(me + d, n)},
                device_id_type=pl.DeviceIdType.MESH,
            )
    pl.semaphore_wait(barrier, sections + tiles - 2)

    def push(way, phase, src, dst):
        n = dict(section=sections, tile=tiles, chip=chips, core=2)[way]
        axis = "section" if way == "section" else "tile"
        send, recv = (sec_send, sec_recv) if way == "section" else (tile_send, tile_recv)
        copies = []
        for d in range(1, n):
            if way == "section":
                peer = lax.rem(sec + d, n)
            elif way == "tile":
                peer = lax.rem(tile + d, n)
            elif way == "chip":
                peer = lax.rem(chip + d, n) * 2 + core
            else:
                peer = chip * 2 + (1 - core)
            copy = pltpu.make_async_remote_copy(
                src_ref=src(peer), dst_ref=dst(d), send_sem=send.at[phase, d],
                recv_sem=recv.at[phase, d], device_id={axis: peer},
                device_id_type=pl.DeviceIdType.MESH,
            )
            copy.start()
            copies.append(copy)
        return copies

    def finish(copies):
        for copy in copies:
            copy.wait()

    side_ref[...] = jnp.zeros_like(side_ref)
    for n, values in enumerate((k_ref[...], weight_ref[...], link_ref[...].astype(F32))):
        side_ref[n * groups : (n + 1) * groups, 0:reaches] = values
    cot_ref[sec, chip, core, 0:slots] = own_ref[...]
    cot_ref[sec, chip, core, slots:] = side_ref[...].T[0:reaches]
    mine = lambda _: cot_ref.at[sec, chip, core]
    moving = push("chip", 6, mine, mine)

    lat_part[...] = jnp.zeros_like(lat_part)
    grads_ref[...] = jnp.zeros_like(grads_ref)
    bias_acc[...] = jnp.zeros_like(bias_acc)

    def onehot(i):
        rows = lax.broadcasted_iota(jnp.int32, (groups * span, block), 0)
        slot = slot_ref[i]
        key = slot + target_ref[i] * reaches
        for g in range(1, groups):
            key = key + jnp.where(slot >= g * reaches, span - reaches, 0)
        return (rows == key).astype(F32).astype(BF16)

    def ahead(i, _):
        at = pl.ds(pl.multiple_of(i * block, block), block)
        pre = jnp.dot(x_ref[at, :], w_in_ref[...], preferred_element_type=F32) + bias_ref[...]
        sig = 0.5 * jnp.tanh(0.5 * pre) + 0.5
        act = pre * sig
        slope_ref[at, :] = (sig + act * (1.0 - sig)).astype(BF16)
        hidden = act.astype(BF16)
        hidden_ref[at, :] = hidden
        runoff = (0.125 * jnp.dot(hidden, w_out_ref[...], preferred_element_type=F32)).astype(BF16)
        part = jnp.dot(onehot(i), runoff, preferred_element_type=F32)
        lat_part[...] += part.reshape(lat_part.shape)
        return 0

    def look(i, _):
        at = pl.ds(pl.multiple_of(i * block, block), block)
        back = jnp.dot(glat_ref[...], onehot(i), preferred_element_type=F32)
        back_ref[at, :] = back.T.astype(BF16)
        grads_ref[0] += jnp.dot(
            back.astype(BF16), hidden_ref[at, :], preferred_element_type=F32
        )
        return 0

    def behind(i, _):
        at = pl.ds(pl.multiple_of(i * block, block), block)
        grad_hidden = lax.dot_general(
            back_ref[at, :], w_out_ref[...], (((1,), (1,)), ((), ())), preferred_element_type=F32
        )
        grad_pre = grad_hidden * slope_ref[at, :].astype(F32)
        bias_acc[...] += jnp.sum(grad_pre, axis=0, keepdims=True)
        grads_ref[1] += jnp.dot(x_ref[at, :].T, grad_pre.astype(BF16), preferred_element_type=F32)
        return 0

    part_of = lambda k: n_blocks * k // 16
    lax.fori_loop(0, part_of(4), ahead, 0)
    finish(moving)
    mine = lambda _: cot_ref.at[sec, :, core]
    moving = push("section", 0, mine, mine)
    lax.fori_loop(part_of(4), part_of(13), ahead, 0)
    finish(moving)
    mine = lambda _: cot_ref.at[:, :, core]
    moving = push("core", 7, mine, mine)
    lax.fori_loop(part_of(13), n_blocks, ahead, 0)
    finish(moving)
    moving = push("tile", 0, lambda peer: lat_part.at[:, peer], lambda d: lat_ref.at[d])

    rows = lambda s: cot_ref[s, :, :, slots:, :].reshape(span, steps).T

    def emit_glat(s, glat):
        @pl.when(sec == s)
        def _():
            glat_ref[...] = (0.125 * glat.astype(BF16).astype(F32)).astype(BF16)

    adjoint_chain(
        rows,
        lambda g, s: cot_ref[s, :, :, g * reaches : (g + 1) * reaches, :].reshape(span, steps),
        groups, sections, span, emit_glat,
    )

    finish(moving)
    total = lat_part[:, tile]
    for d in range(1, tiles):
        total = total + lat_ref[d]
    lat_all[sec, chip, core] = total
    mine = lambda _: lat_all.at[sec, chip, core]
    laterals = push("chip", 8, mine, mine)
    lax.fori_loop(0, part_of(8), look, 0)
    finish(laterals)
    mine_sec = lambda _: lat_all.at[sec, :, core]
    laterals = push("section", 1, mine_sec, mine_sec)
    lax.fori_loop(part_of(8), n_blocks, look, 0)

    def scatter_sections(k, phase):
        for s in range(sections):
            for t in range(tiles):
                ws_ref[k, s, t] = grads_ref[(k,) + spot(wg, hid, s * tiles + t)].astype(BF16)
        return push(
            "section", phase, lambda peer: ws_ref.at[k, peer], lambda d: wr1.at[k, d]
        )

    def scatter_tiles(k, phase):
        total = ws_ref[k, sec].astype(F32)
        for d in range(1, sections):
            total = total + wr1[k, d].astype(F32)
        ws2[k] = total
        return push("tile", phase, lambda peer: ws2.at[k, peer], lambda d: wr2.at[k, d])

    def gather_tiles(k, phase):
        total = ws2[k, tile]
        for d in range(1, tiles):
            total = total + wr2[k, d]
        wg[k, sec, tile] = total.astype(BF16)
        mine = lambda _: wg.at[k, sec, tile]
        return push("tile", phase, mine, mine)

    def gather_sections(k, phase):
        mine = lambda _: wg.at[k, sec]
        return push("section", phase, mine, mine)

    moving = scatter_sections(0, 2)
    lax.fori_loop(0, part_of(5), behind, 0)
    finish(laterals)
    mine_core = lambda _: lat_all.at[:, :, core]
    laterals = push("core", 9, mine_core, mine_core)
    finish(moving)
    moving = scatter_tiles(0, 1)
    lax.fori_loop(part_of(5), part_of(9), behind, 0)
    finish(laterals)
    finish(moving)
    moving = gather_tiles(0, 2)
    lax.fori_loop(part_of(9), part_of(12), behind, 0)
    finish(moving)
    outer = gather_sections(0, 3)
    lax.fori_loop(part_of(12), n_blocks, behind, 0)

    moving = scatter_sections(1, 4)
    moving += push("section", 5, lambda _: bias_acc, lambda d: br1.at[d])

    def emit_flow(s, flow):
        @pl.when(sec == s)
        def _():
            for g in range(groups):
                flow_ref[g] = flow[:, g * span : (g + 1) * span].T.reshape(tiles, reaches, steps)

    forward_chain(
        rows,
        lambda g, s: lat_all[s, :, :, g].reshape(span, steps),
        groups, sections, span, emit_flow,
    )
    flow_out[...] = flow_ref[:, tile]

    finish(outer)
    finish(moving)
    bias = bias_acc[...]
    for d in range(1, sections):
        bias = bias + br1[d]
    bias_sum[...] = bias
    moving = scatter_tiles(1, 3)
    moving += push("tile", 5, lambda _: bias_sum, lambda d: br2.at[d])
    finish(moving)
    moving = gather_tiles(1, 4)
    for d in range(1, tiles):
        bias = bias + br2[d]
    bias_out[...] = bias
    wg_out[0] = wg[0]
    finish(moving)
    moving = gather_sections(1, 6)
    finish(moving)
    wg_out[1] = wg[1]


def spot(chunks, hid, c):
    chunk_rows, chunk_cols = chunks.shape[3:]
    col_split = hid // chunk_cols
    r, w = c // col_split * chunk_rows, c % col_split * chunk_cols
    return slice(r, r + chunk_rows), slice(w, w + chunk_cols)


def unpack_kernel(flow_ref, bias_ref, wg_ref, flow_out, w_in_out, bias_out, w_out_out, turned):
    _, sections, tiles = wg_ref.shape[:3]
    hid = w_in_out.shape[1]
    for s in range(sections):
        for t in range(tiles):
            where = spot(wg_ref, hid, s * tiles + t)
            turned[where] = wg_ref[0, s, t].astype(F32)
            w_in_out[where] = wg_ref[1, s, t].astype(F32)
    w_out_out[...] = turned[...].T
    flow_out[...] = flow_ref[...]
    bias_out[...] = bias_ref[...]


def local(
    forcing, w_in, bias_in, w_out, target_tile_index, reach_slot,
    k_ratio, x_weight, down_link, cotangent,
):
    tiles = lax.axis_size("tile")
    sections = lax.axis_size("section")
    cells, feat = forcing.shape
    hid, steps = w_out.shape
    groups, reaches = k_ratio.shape
    span = tiles * reaches
    slots = groups * reaches
    chips = tiles // 2
    block = min(cells // 2, 512)
    chunk_rows = 8
    chunk_cols = feat * hid // (sections * tiles * chunk_rows)

    vmem = pl.BlockSpec(memory_space=pltpu.VMEM)
    part = (chunk_rows, chunk_cols)
    flow, g_bias, packed = pl.pallas_call(
        functools.partial(step_kernel, groups, sections, tiles, reaches, block),
        in_specs=[vmem] * 10,
        out_specs=[vmem] * 3,
        out_shape=[
            jax.ShapeDtypeStruct((groups, reaches, steps), F32),
            jax.ShapeDtypeStruct((1, hid), F32),
            jax.ShapeDtypeStruct((2, sections, tiles) + part, BF16),
        ],
        scratch_shapes=[
            pltpu.VMEM((steps, steps), F32),
            pltpu.VMEM((cells, hid), BF16),
            pltpu.VMEM((cells, hid), BF16),
            pltpu.VMEM((cells, steps), BF16),
            pltpu.VMEM((sections, chips, 2, slots + reaches, steps), F32),
            pltpu.VMEM((tiles, groups, reaches, steps), F32),
            pltpu.VMEM((groups, tiles, reaches, steps), F32),
            pltpu.VMEM((sections, chips, 2, groups, reaches, steps), F32),
            pltpu.VMEM((steps, groups * span), BF16),
            pltpu.VMEM((2, feat, hid), F32),
            pltpu.VMEM((1, hid), F32),
            pltpu.VMEM((groups, tiles, reaches, steps), F32),
            pltpu.VMEM((2, sections, tiles) + part, BF16),
            pltpu.VMEM((2, sections, tiles) + part, BF16),
            pltpu.VMEM((2, tiles) + part, F32),
            pltpu.VMEM((2, tiles) + part, F32),
            pltpu.VMEM((2, sections, tiles) + part, BF16),
            pltpu.VMEM((sections, 1, hid), F32),
            pltpu.VMEM((tiles, 1, hid), F32),
            pltpu.VMEM((1, hid), F32),
            pltpu.SemaphoreType.DMA((7, sections)),
            pltpu.SemaphoreType.DMA((7, sections)),
            pltpu.SemaphoreType.DMA((10, tiles)),
            pltpu.SemaphoreType.DMA((10, tiles)),
        ],
        compiler_params=pltpu.CompilerParams(
            vmem_limit_bytes=60 << 20, collective_id=0, has_side_effects=True
        ),
    )(
        forcing, target_tile_index.reshape(cells // block, 1, block),
        reach_slot.reshape(cells // block, 1, block), w_in, bias_in[None, :], w_out,
        k_ratio, x_weight, down_link, cotangent.reshape(slots, steps),
    )
    flow, g_in, g_bias, g_out = pl.pallas_call(
        unpack_kernel,
        in_specs=[vmem] * 3,
        out_specs=[vmem] * 4,
        out_shape=[
            jax.ShapeDtypeStruct((groups, reaches, steps), F32),
            jax.ShapeDtypeStruct((feat, hid), F32),
            jax.ShapeDtypeStruct((1, hid), F32),
            jax.ShapeDtypeStruct((hid, steps), F32),
        ],
        scratch_shapes=[pltpu.VMEM((steps, hid), F32)],
    )(flow, g_bias, packed)
    return (flow, g_in, g_bias[0], g_out)


def solution(mesh):
    placed = (
        P(("section", "tile"), None),
        P(),
        P(),
        P(),
        P(("section", "tile"), None),
        P(("section", "tile")),
        P(None, ("section", "tile")),
        P(None, ("section", "tile")),
        P(None, ("section", "tile")),
        P(None, ("section", "tile"), None),
    )
    return jax.shard_map(
        local,
        mesh=mesh,
        in_specs=placed,
        out_specs=(P(None, ("section", "tile"), None), P(), P(), P()),
        check_vma=False,
    )
```

time: 103 us -> 87.8 us (0.85)
  local copies, waits for them, and re-layouts: 8 us -> 0 us
  other arithmetic: 4.34 us -> 0 us
  Pallas kernels: 89.8 us -> 87 us
    unnamed x6 -> x0, local copies, waits for them, and re-layouts: 7.91 us -> none
    pallas_call x1, Pallas kernels: 89.8 us -> 84.9 us  [local(): pl.pallas_call(functools.partial(step_kernel, groups, sections, tiles, re...]
    pallas_call x0 -> x1, Pallas kernels: none -> 2.15 us  [local(): pl.pallas_call(unpack_kernel, in_specs=[vmem] * 3, out_specs=[vmem] * 4,...]
    add x1 -> x0, other arithmetic: 1.41 us -> none  [local(): reach_slot // reaches * span + target_tile_index[:, 0] * reaches]
    concatenate x1 -> x0, other arithmetic: 1.38 us -> none  [local(): own = jnp.concatenate([cotangent.reshape(slots, steps), own], axis=0)]
where the time goes in v3:
time: 87.8 us; the launch traced here: 87.7 us
  Pallas kernels  87 us (99%)
    pallas_call x1, Pallas kernels, local(): pl.pallas_call(functools.partial(step_kernel, groups, sections, tiles, re...  84.9 us
    pallas_call x1, Pallas kernels, local(): pl.pallas_call(unpack_kernel, in_specs=[vmem] * 3, out_specs=[vmem] * 4,...  2.15 us

profile of v3, /device:TPU:0, one launch (start us, length us, event | category | flops | bytes accessed | tf_op | source)
XLA Modules:
  0.0 87.7 jit_solution(15554081442828394146)
XLA Ops:
  0.6 84.9 %shard_map.129 = (f32[4,16,128]{2,1,0:T(8,128)}, f32[1,1024]{1,0:T(1,128)}, bf16[2,4,8,8,512]{4,3,2,1,0:T(8,128)(2,1)}) custom-call(bf16[8192,128]{1,0:T(8,128)(2,1)} %x_ref.1, s32[16,1,512]{2,1,0:T(1,128)} %bitcast.5, s32[16,1,512]{2,1,0:T(1,128)} %bitcast.6, bf16[128,1024]{1,0:T(8,128)(2,1)} %w_in_ref.1, f32[1,1024]{1,0:T(1,128)} %bitcast.8, ...), custom_call_target="tpu_custom_call" | custom-call | tf_op jit(solution)/shard_map/pallas_call | solution.py:361
  85.5 2.1 %shard_map.130 = (f32[4,16,128]{2,1,0:T(8,128)}, f32[128,1024]{1,0:T(8,128)}, f32[1,1024]{1,0:T(1,128)}, f32[1024,128]{1,0:T(8,128)}) custom-call(f32[4,16,128]{2,1,0:T(8,128)} %get-tuple-element.11.flow_ref, f32[1,1024]{1,0:T(1,128)} %get-tuple-element.12.bias_ref, bf16[2,4,8,8,512]{4,3,2,1,0:T(8,128)(2,1)} %get-tuple-element.13.wg_ref), custom_call_target="tpu_custom_call" | custom-call | tf_op jit(solution)/shard_map/pallas_call | solution.py:404

commit v4 on v3

--- a/solution.py
+++ b/solution.py
@@ -352,7 +352,7 @@
     span = tiles * reaches
     slots = groups * reaches
     chips = tiles // 2
-    block = min(cells // 2, 512)
+    block = min(cells // 2, 1024 if groups * span <= 512 else 512)
     chunk_rows = 8
     chunk_cols = feat * hid // (sections * tiles * chunk_rows)
 

time: 87.8 us -> 83.1 us (0.946)
  Pallas kernels: 87 us -> 82.3 us
    pallas_call x1, Pallas kernels: 84.9 us -> 80.1 us  [local(): pl.pallas_call(functools.partial(step_kernel, groups, sections, tiles, re...]
where the time goes in v4:
time: 83.1 us; the launch traced here: 82.9 us
  Pallas kernels  82.3 us (99%)
    pallas_call x1, Pallas kernels, local(): pl.pallas_call(functools.partial(step_kernel, groups, sections, tiles, re...  80.1 us
    pallas_call x1, Pallas kernels, local(): pl.pallas_call(unpack_kernel, in_specs=[vmem] * 3, out_specs=[vmem] * 4,...  2.15 us

profile of v4, /device:TPU:0, one launch (start us, length us, event | category | flops | bytes accessed | tf_op | source)
XLA Modules:
  0.0 82.9 jit_solution(13336748482886654716)
XLA Ops:
  0.6 80.1 %shard_map.129 = (f32[4,16,128]{2,1,0:T(8,128)}, f32[1,1024]{1,0:T(1,128)}, bf16[2,4,8,8,512]{4,3,2,1,0:T(8,128)(2,1)}) custom-call(bf16[8192,128]{1,0:T(8,128)(2,1)} %x_ref.1, s32[8,1,1024]{2,1,0:T(1,128)} %bitcast.5, s32[8,1,1024]{2,1,0:T(1,128)} %bitcast.6, bf16[128,1024]{1,0:T(8,128)(2,1)} %w_in_ref.1, f32[1,1024]{1,0:T(1,128)} %bitcast.8, ...), custom_call_target="tpu_custom_call" | custom-call | tf_op jit(solution)/shard_map/pallas_call | solution.py:361
  80.8 2.1 %shard_map.130 = (f32[4,16,128]{2,1,0:T(8,128)}, f32[128,1024]{1,0:T(8,128)}, f32[1,1024]{1,0:T(1,128)}, f32[1024,128]{1,0:T(8,128)}) custom-call(f32[4,16,128]{2,1,0:T(8,128)} %get-tuple-element.11.flow_ref, f32[1,1024]{1,0:T(1,128)} %get-tuple-element.12.bias_ref, bf16[2,4,8,8,512]{4,3,2,1,0:T(8,128)(2,1)} %get-tuple-element.13.wg_ref), custom_call_target="tpu_custom_call" | custom-call | tf_op jit(solution)/shard_map/pallas_call | solution.py:404
